TPU v7x, 32 devices: a whole 2x2x4 slice. The times are simulated.
32 devices in a mesh: dp: 8 (over y, x, core), dap: 4 (over z).
Axes of the slice: x: 2, y: 2, z: 4, core: 2. Of those that a mesh axis runs over, the one named last changes fastest.
Arguments:
- pair_act: bfloat16 [8, 128, 128, 128], P('dp', 'dap'), may hold values from -6 to 6
- pair_cot: bfloat16 [8, 128, 128, 128], P('dp', 'dap'), may hold values from -6 to 6
- in_gain: float32 [128], replicated, may hold values from 0.25 to 1.75
- in_bias: float32 [128], replicated, may hold values from -3 to 3
- proj_weight: bfloat16 [128, 512], replicated, may hold values from -0.5 to 0.5
- gate_weight: bfloat16 [128, 128], replicated, may hold values from -0.5 to 0.5
- out_gain: float32 [128], replicated, may hold values from 0.25 to 1.75
- out_bias: float32 [128], replicated, may hold values from -3 to 3
- out_weight: bfloat16 [128, 128], replicated, may hold values from -0.5 to 0.5
Outputs:
- update: bfloat16 [8, 128, 128, 128], P('dp', 'dap')
- pair_grad: bfloat16 [8, 128, 128, 128], P('dp', 'dap')
- proj_grad: float32 [128, 512], replicated
- gate_grad: float32 [128, 128], replicated
- out_grad: float32 [128, 128], replicated
- in_norm_grad: float32 [2, 128], replicated
- out_norm_grad: float32 [2, 128], replicated
All inputs are finite; a program needn't handle non-finite values.
Results may differ from a plain program's by a relative error of at most 0.0084.
Values may be sent and summed in bfloat16 or wider, within the bound.
A program may use at most 64 MiB of HBM per device.

v0:
```python
import jax
import jax.numpy as jnp
from jax import lax
from jax.sharding import PartitionSpec as P

epsilon = 1e-05


def norm_rows(values, along):
    row_mean = jnp.mean(values, axis=along, keepdims=True)
    centred = values - row_mean
    row_var = jnp.mean(centred * centred, axis=along, keepdims=True)
    inv_std = lax.rsqrt(row_var + epsilon)
    return (centred * inv_std, inv_std)


def norm_back(grad_hat, x_hat, inv_std, along):
    first = jnp.mean(grad_hat, axis=along, keepdims=True)
    second = jnp.mean(grad_hat * x_hat, axis=along, keepdims=True)
    return (grad_hat - first - x_hat * second) * inv_std


def backward_pieces(piece_d, piece_l, piece_r):
    back_l = jnp.einsum(
        "zhij,zhjk->zhik", piece_d, piece_r, preferred_element_type=jnp.float32
    ).astype(jnp.bfloat16)
    back_r = jnp.einsum(
        "zhij,zhik->zhjk", piece_d, piece_l, preferred_element_type=jnp.float32
    ).astype(jnp.bfloat16)
    return (back_l, back_r)


def shards(
    pair_act, pair_cot, in_gain, in_bias, proj_weight, gate_weight, out_gain, out_bias, out_weight
):
    f32 = jnp.float32
    bf16 = jnp.bfloat16
    groups = lax.axis_size("dap")
    row_count = pair_act.shape[1]
    crop_len = pair_act.shape[2]
    channels = pair_act.shape[3]
    hidden_w = out_weight.shape[0]
    per_dev = hidden_w // groups
    cell_count = row_count * crop_len
    scale = 1.0 / crop_len
    flat_act = pair_act.reshape(cell_count, channels).astype(f32)
    in_hat, in_inv = norm_rows(flat_act, 1)
    normed = (in_hat * in_gain + in_bias).astype(bf16)
    projected = jnp.einsum("mc,ch->hm", normed, proj_weight, preferred_element_type=f32)
    pre_ag = projected[0:hidden_w]
    pre_ap = projected[hidden_w : 2 * hidden_w]
    pre_bg = projected[2 * hidden_w : 3 * hidden_w]
    pre_bp = projected[3 * hidden_w : 4 * hidden_w]
    sig_a = jax.nn.sigmoid(pre_ag)
    sig_b = jax.nn.sigmoid(pre_bg)
    left_act = (sig_a * pre_ap).astype(bf16).reshape(groups, per_dev, row_count, crop_len)
    right_act = (sig_b * pre_bp).astype(bf16).reshape(groups, per_dev, row_count, crop_len)
    piece_l = lax.all_to_all(left_act, "dap", split_axis=0, concat_axis=2, tiled=True)
    piece_r = lax.all_to_all(right_act, "dap", split_axis=0, concat_axis=2, tiled=True)
    product = jnp.einsum("zhik,zhjk->zhij", piece_l, piece_r, preferred_element_type=f32).astype(
        bf16
    )
    returned = lax.all_to_all(product, "dap", split_axis=2, concat_axis=0, tiled=True)
    tri_out = returned.reshape(hidden_w, cell_count)
    tri_hat, tri_inv = norm_rows(tri_out.astype(f32), 0)
    tri_norm = (tri_hat * out_gain[:, None] + out_bias[:, None]).astype(bf16)
    gate_val = jax.nn.sigmoid(jnp.dot(normed, gate_weight, preferred_element_type=f32))
    mixed = jnp.einsum("hm,hc->mc", tri_norm, out_weight, preferred_element_type=f32)
    update = (gate_val * mixed).astype(bf16).reshape(1, row_count, crop_len, channels)
    cot_flat = pair_cot.reshape(cell_count, channels).astype(f32)
    d_mixed = (cot_flat * gate_val).astype(bf16)
    d_gate = (cot_flat * mixed * gate_val * (1.0 - gate_val)).astype(bf16)
    out_part = jnp.einsum("hm,mc->hc", tri_norm, d_mixed, preferred_element_type=f32) * scale
    gate_part = jnp.einsum("mc,md->cd", normed, d_gate, preferred_element_type=f32) * scale
    d_norm_out = jnp.einsum("mc,hc->hm", d_mixed, out_weight, preferred_element_type=f32)
    out_norm_part = (
        jnp.stack([jnp.sum(d_norm_out * tri_hat, axis=1), jnp.sum(d_norm_out, axis=1)]) * scale
    )
    d_tri = norm_back(d_norm_out * out_gain[:, None], tri_hat, tri_inv, 0).astype(bf16)
    d_tri = d_tri.reshape(groups, per_dev, row_count, crop_len)
    d_cols = lax.all_to_all(d_tri, "dap", split_axis=0, concat_axis=2, tiled=True)
    back_l, back_r = backward_pieces(d_cols, piece_l, piece_r)
    d_left, d_right = (
        lax.all_to_all(back_l, "dap", split_axis=2, concat_axis=0, tiled=True),
        lax.all_to_all(back_r, "dap", split_axis=2, concat_axis=0, tiled=True),
    )
    left_grad = d_left.reshape(hidden_w, cell_count).astype(f32)
    right_grad = d_right.reshape(hidden_w, cell_count).astype(f32)
    d_proj = jnp.concatenate(
        [
            left_grad * pre_ap * sig_a * (1.0 - sig_a),
            left_grad * sig_a,
            right_grad * pre_bp * sig_b * (1.0 - sig_b),
            right_grad * sig_b,
        ],
        axis=0,
    ).astype(bf16)
    proj_part = jnp.einsum("mc,hm->ch", normed, d_proj, preferred_element_type=f32) * scale
    d_normed = jnp.einsum(
        "hm,ch->mc", d_proj, proj_weight, preferred_element_type=f32
    ) + jnp.einsum("md,cd->mc", d_gate, gate_weight, preferred_element_type=f32)
    in_norm_part = (
        jnp.stack([jnp.sum(d_normed * in_hat, axis=0), jnp.sum(d_normed, axis=0)]) * scale
    )
    pair_grad = (
        norm_back(d_normed * in_gain, in_hat, in_inv, 1)
        .astype(bf16)
        .reshape(1, row_count, crop_len, channels)
    )
    proj_sum, gate_sum, out_sum, in_sum, outn_sum = lax.psum(
        (proj_part, gate_part, out_part, in_norm_part, out_norm_part), ("dp", "dap")
    )
    return (update, pair_grad, proj_sum, gate_sum, out_sum, in_sum, outn_sum)


def solution(mesh):
    placed = (
        P("dp", "dap", None, None),
        P("dp", "dap", None, None),
        P(),
        P(),
        P(),
        P(),
        P(),
        P(),
        P(),
    )
    return jax.shard_map(
        shards,
        mesh=mesh,
        in_specs=placed,
        out_specs=(P("dp", "dap", None, None), P("dp", "dap", None, None), P(), P(), P(), P(), P()),
        check_vma=False,
    )
```

profile of v0, /device:TPU:0, one launch (start us, length us, event | category | flops | bytes accessed | tf_op | source)
XLA Modules:
  0.0 383.8 jit_solution(13851624344998094155)
XLA Ops:
  7.2 1.7 convert_reduce_fusion
  8.9 2.3 multiply_reduce_fusion.3
  11.3 1.3 add_convert_fusion.1
  12.6 1.0 copy-done.5
  13.5 1.3 convolution_bitcast_fusion
  14.8 1.1 fusion.30
  15.9 2.1 copy-done.1
  18.1 1.2 copy.46
  19.3 6.3 %all-to-all-start.1 = ((bf16[4,32,32,128]{3,2,1,0:T(8,128)(2,1)}), bf16[4,32,32,128]{3,2,1,0:T(8,128)(2,1)S(1)}, u32[]{:S(2)}, u32[]{:S(2)}) async-start(bf16[4,32,32,128]{3,2,1,0:T(8,128)(2,1)} %bitcast.157), calls=%async_computation.1 | async-start | bytes 2097152 | tf_op jit(solution)/shard_map/all_to_all | solution.py:59
  25.6 1.2 copy.45
  26.8 24.5 %all-to-all-done.1 = bf16[4,32,32,128]{3,2,1,0:T(8,128)(2,1)S(1)} async-done(((bf16[4,32,32,128]{3,2,1,0:T(8,128)(2,1)}), bf16[4,32,32,128]{3,2,1,0:T(8,128)(2,1)S(1)}, u32[]{:S(2)}, u32[]{:S(2)}) %all-to-all-start.1) | async-done | bytes 1048608 | tf_op jit(solution)/shard_map/all_to_all | solution.py:59
  51.4 4.3 %all-to-all-start = ((bf16[4,32,32,128]{3,2,1,0:T(8,128)(2,1)}), bf16[4,32,32,128]{3,2,1,0:T(8,128)(2,1)}, u32[]{:S(2)}, u32[]{:S(2)}) async-start(bf16[4,32,32,128]{3,2,1,0:T(8,128)(2,1)} %bitcast.156), calls=%async_computation | async-start | bytes 2097152 | tf_op jit(solution)/shard_map/all_to_all | solution.py:58
  55.8 25.2 %all-to-all-done = bf16[4,32,32,128]{3,2,1,0:T(8,128)(2,1)} async-done(((bf16[4,32,32,128]{3,2,1,0:T(8,128)(2,1)}), bf16[4,32,32,128]{3,2,1,0:T(8,128)(2,1)}, u32[]{:S(2)}, u32[]{:S(2)}) %all-to-all-start) | async-done | bytes 1048608 | tf_op jit(solution)/shard_map/all_to_all | solution.py:58
  81.0 1.3 copy.32
  83.9 27.7 %all_to_all.72 = bf16[1,32,128,128]{3,1,0,2:T(8,128)(2,1)S(1)} all-to-all(bf16[1,32,128,128]{3,1,0,2:T(8,128)(2,1)S(1)} %copy.34), channel_id=1, replica_groups=mesh['dp'=8,'dap'=4] {'dap'}, dimensions={2} | all-to-all | bytes 2097152 | tf_op jit(solution)/shard_map/all_to_all | solution.py:63
  112.2 1.1 bitcast_reduce_fusion
  113.4 1.1 fusion.23
  114.5 3.0 copy.58
  117.5 1.9 copy.36
  119.4 2.3 add_convert_fusion
  121.8 1.0 copy-done.12
  124.3 2.7 fusion.6
  127.0 2.4 fusion.21
  129.4 1.3 copy-done.3
  130.8 4.1 %multiply_convert_fusion.1 = bf16[128,4096]{0,1:T(8,128)(2,1)} fusion(f32[4096,128]{1,0:T(8,128)S(1)} %get-tuple-element.34, f32[128,4096]{0,1:T(8,128)S(1)} %copy.36, f32[4096]{0:T(1024)S(1)} %get-tuple-element.36, f32[4096]{0:T(1024)S(1)} %get-tuple-element.37, f32[128]{0:T(128)S(1)} %copy-done.22, f32[4096]{0:T(1024)S(1)} %rsqrt_bitcast_fusion, ...), kind=kLoop, calls=%fused_computation.46 | loop fusion | flops 4194304 | bytes 5308928 | tf_op jit(solution)/shard_map/convert_element_type | solution.py:79
  134.8 1.5 copy.37
  136.6 27.8 %all_to_all.73 = bf16[4,32,32,128]{3,2,1,0:T(8,128)(2,1)S(1)} all-to-all(bf16[4,32,32,128]{3,2,1,0:T(8,128)(2,1)S(1)} %bitcast.159), channel_id=1, replica_groups=mesh['dp'=8,'dap'=4] {'dap'}, dimensions={0} | all-to-all | bytes 2097152 | tf_op jit(solution)/shard_map/all_to_all | solution.py:81
  165.0 1.7 copy.39
  166.6 4.3 %all-to-all-start.4 = ((bf16[1,32,128,128]{3,1,0,2:T(8,128)(2,1)}), bf16[1,32,128,128]{3,1,0,2:T(8,128)(2,1)}, u32[]{:S(2)}, u32[]{:S(2)}) async-start(bf16[1,32,128,128]{3,1,0,2:T(8,128)(2,1)} %copy.39), calls=%async_computation.4 | async-start | bytes 2097152 | tf_op jit(solution)/shard_map/all_to_all | solution.py:84
  171.4 1.7 copy.42
  173.1 22.6 %all-to-all-done.4 = bf16[1,32,128,128]{3,1,0,2:T(8,128)(2,1)} async-done(((bf16[1,32,128,128]{3,1,0,2:T(8,128)(2,1)}), bf16[1,32,128,128]{3,1,0,2:T(8,128)(2,1)}, u32[]{:S(2)}, u32[]{:S(2)}) %all-to-all-start.4) | async-done | bytes 1048608 | tf_op jit(solution)/shard_map/all_to_all | solution.py:84
  195.7 4.5 %all-to-all-start.5 = ((bf16[1,32,128,128]{3,1,0,2:T(8,128)(2,1)}), bf16[1,32,128,128]{3,1,0,2:T(8,128)(2,1)}, u32[]{:S(2)}, u32[]{:S(2)}) async-start(bf16[1,32,128,128]{3,1,0,2:T(8,128)(2,1)} %copy.42), calls=%async_computation.5 | async-start | bytes 2097152 | tf_op jit(solution)/shard_map/all_to_all | solution.py:85
  200.8 2.8 convolution_multiply_fusion.1
  203.6 1.1 convolution_multiply_fusion.2
  204.7 2.9 copy.40
  207.7 17.9 %all-to-all-done.5 = bf16[1,32,128,128]{3,1,0,2:T(8,128)(2,1)} async-done(((bf16[1,32,128,128]{3,1,0,2:T(8,128)(2,1)}), bf16[1,32,128,128]{3,1,0,2:T(8,128)(2,1)}, u32[]{:S(2)}, u32[]{:S(2)}) %all-to-all-start.5) | async-done | bytes 1048608 | tf_op jit(solution)/shard_map/all_to_all | solution.py:85
  225.5 1.7 copy.43
  227.4 6.3 %fusion.13 = (bf16[128,4096]{1,0:T(8,128)(2,1)S(1)}, bf16[128,4096]{1,0:T(8,128)(2,1)S(1)}, bf16[128,4096]{1,0:T(8,128)(2,1)S(1)}, bf16[128,4096]{1,0:T(8,128)(2,1)S(1)}) fusion(f32[16,8,32,128]{3,2,1,0:T(8,128)S(1)} %bitcast.153, f32[512,4096]{1,0:T(8,128)} %copy-done.1, f32[16,8,32,128]{3,2,1,0:T(8,128)S(1)} %bitcast.154), kind=kLoop, calls=%fused_computation.23 | loop fusion | flops 10485760 | bytes 16777216 | tf_op jit(solution)/shard_map/convert.13
  233.8 1.0 copy-done.17
  235.4 2.2 convolution_multiply_fusion
  237.6 3.0 fusion.31
  240.6 2.4 multiply_reduce_fusion
  243.1 3.3 multiply_convert_fusion
  246.3 37.9 %all-reduce = (f32[2,128]{1,0:T(2,128)}, f32[2,128]{1,0:T(2,128)}) all-reduce(f32[2,128]{1,0:T(2,128)S(1)} %maximum_multiply_fusion, f32[2,128]{1,0:T(2,128)S(1)} %maximum_multiply_fusion.1), channel_id=1, replica_groups=mesh['dp'=8,'dap'=4] {'dp','dap'}, use_global_device_ids=true, to_apply=%region_13.0 | all-reduce | flops 512 | bytes 4096 | tf_op jit(solution)/shard_map/psum | solution.py:110
  284.3 88.0 %all-reduce.4.cloned.1.call-done = (f32[128,512]{1,0:T(8,128)}, f32[128,128]{1,0:T(8,128)}, f32[128,128]{1,0:T(8,128)}) async-done(((f32[128,512]{1,0:T(8,128)}, f32[128,128]{1,0:T(8,128)}, f32[128,128]{1,0:T(8,128)}), (f32[128,512]{1,0:T(8,128)}, f32[128,128]{1,0:T(8,128)}, f32[128,128]{1,0:T(8,128)})) %all-reduce.4.cloned.1.call-update) | async-done | bytes 393232 | tf_op jit(solution)/shard_map/psum | solution.py:110
  372.3 1.7 copy.62
  374.0 1.5 copy.63
  375.5 1.5 copy.64
  (71 shorter events, 6.8 us)
Async XLA Ops:
  7.2 6.4 %copy-start = (bf16[128,512]{1,0:T(8,128)(2,1)S(1)}, bf16[128,512]{1,0:T(8,128)(2,1)}, u32[]{:S(2)}) copy-start(bf16[128,512]{1,0:T(8,128)(2,1)} %param.13) | copy-start | bytes 393220
  7.2 4.1 %copy-start.2 = (bf16[1,32,128,128]{3,2,1,0:T(8,128)(2,1)S(1)}, bf16[1,32,128,128]{3,2,1,0:T(8,128)(2,1)}, u32[]{:S(2)}) copy-start(bf16[1,32,128,128]{3,2,1,0:T(8,128)(2,1)} %param.9) | copy-start | bytes 3145732
  7.2 4.1 %copy-start.23 = (f32[128]{0:T(128)S(1)}, f32[128]{0:T(128)}, u32[]{:S(2)}) copy-start(f32[128]{0:T(128)} %param.11) | copy-start | bytes 1540
  7.2 4.1 %copy-start.25 = (f32[128]{0:T(128)S(1)}, f32[128]{0:T(128)}, u32[]{:S(2)}) copy-start(f32[128]{0:T(128)} %param.12) | copy-start | bytes 1540
  12.6 1.0 copy-start.5
  14.8 3.2 copy-start.1
  19.3 32.1 %all-to-all-start.1 = ((bf16[4,32,32,128]{3,2,1,0:T(8,128)(2,1)}), bf16[4,32,32,128]{3,2,1,0:T(8,128)(2,1)S(1)}, u32[]{:S(2)}, u32[]{:S(2)}) async-start(bf16[4,32,32,128]{3,2,1,0:T(8,128)(2,1)} %bitcast.157), calls=%async_computation.1 | async-start | bytes 2097152 | tf_op jit(solution)/shard_map/all_to_all | solution.py:59
  51.4 29.6 %all-to-all-start = ((bf16[4,32,32,128]{3,2,1,0:T(8,128)(2,1)}), bf16[4,32,32,128]{3,2,1,0:T(8,128)(2,1)}, u32[]{:S(2)}, u32[]{:S(2)}) async-start(bf16[4,32,32,128]{3,2,1,0:T(8,128)(2,1)} %bitcast.156), calls=%async_computation | async-start | bytes 2097152 | tf_op jit(solution)/shard_map/all_to_all | solution.py:58
  55.8 27.4 %copy-start.10 = (bf16[1,32,4,32,128]{4,3,2,1,0:T(8,128)(2,1)}, bf16[1,32,4,32,128]{4,3,2,1,0:T(8,128)(2,1)S(1)}, u32[]{:S(2)}) copy-start(bf16[1,32,4,32,128]{4,3,2,1,0:T(8,128)(2,1)S(1)} %copy.33) | copy-start | bytes 3145732
  82.3 1.6 copy-start.8
  117.5 2.0 copy-start.22
  117.5 2.0 copy-start.24
  119.4 3.3 copy-start.20
  121.7 1.0 copy-start.12
  122.7 1.2 copy-start.6
  122.7 1.2 copy-start.21
  122.8 1.6 copy-start.26
  127.0 2.4 copy-start.16
  129.4 1.4 copy-start.3
  136.6 27.9 %copy-start.11 = (bf16[1,32,4,32,128]{4,3,2,1,0:T(8,128)(2,1)S(1)}, bf16[1,32,4,32,128]{4,3,2,1,0:T(8,128)(2,1)}, u32[]{:S(2)}) copy-start(bf16[1,32,4,32,128]{4,3,2,1,0:T(8,128)(2,1)} %copy-done.10) | copy-start | bytes 3145732
  165.0 5.9 %copy-start.9 = (bf16[1,32,4,32,128]{4,3,2,1,0:T(8,128)(2,1)S(1)}, bf16[1,32,4,32,128]{4,3,2,1,0:T(8,128)(2,1)}, u32[]{:S(2)}) copy-start(bf16[1,32,4,32,128]{4,3,2,1,0:T(8,128)(2,1)} %copy-done.8) | copy-start | bytes 3145732
  166.6 29.1 %all-to-all-start.4 = ((bf16[1,32,128,128]{3,1,0,2:T(8,128)(2,1)}), bf16[1,32,128,128]{3,1,0,2:T(8,128)(2,1)}, u32[]{:S(2)}, u32[]{:S(2)}) async-start(bf16[1,32,128,128]{3,1,0,2:T(8,128)(2,1)} %copy.39), calls=%async_computation.4 | async-start | bytes 2097152 | tf_op jit(solution)/shard_map/all_to_all | solution.py:84
  171.4 28.8 %copy-start.4 = (f32[4096,128]{1,0:T(8,128)S(1)}, f32[4096,128]{1,0:T(8,128)}, u32[]{:S(2)}) copy-start(f32[4096,128]{1,0:T(8,128)} %copy-done.3) | copy-start | bytes 6291460
  195.7 29.8 %all-to-all-start.5 = ((bf16[1,32,128,128]{3,1,0,2:T(8,128)(2,1)}), bf16[1,32,128,128]{3,1,0,2:T(8,128)(2,1)}, u32[]{:S(2)}, u32[]{:S(2)}) async-start(bf16[1,32,128,128]{3,1,0,2:T(8,128)(2,1)} %copy.42), calls=%async_computation.5 | async-start | bytes 2097152 | tf_op jit(solution)/shard_map/all_to_all | solution.py:85
  200.2 172.1 %all-reduce.4.cloned.1.call-start = ((), (), s32[]{:S(2)}) async-start(), calls=%async_computation.6 | async-start | bytes 786432 | tf_op jit(solution)/shard_map/psum | solution.py:110
  200.8 2.8 copy-start.7
  200.8 2.8 copy-start.14
  225.5 1.9 copy-start.13
  233.7 1.0 copy-start.17
  233.8 1.3 copy-start.18
  233.8 1.6 copy-start.19
  237.6 3.0 copy-start.15
Sparse Core Ops, SparseCore 0:
  243.2 129.0 all-reduce.3
where the time goes:
time: 385 us; the launch traced here: 384 us
  waiting for transfers between devices  178 us (46%)
  blocking collectives  93.5 us (24%)
  local copies, waits for them, and re-layouts  32.7 us (8%)
  other arithmetic  25.3 us (7%)
  matrix products  20.1 us (5%)
  starting transfers between devices  19.4 us (5%)
  between operations  14.6 us (4%)
    psum x1, waiting for transfers between devices, shards(): lax.psum((proj_part, gate_part, out_part, in_norm_part, out_norm_part), (...  88 us
    psum x1, blocking collectives, shards(): lax.psum((proj_part, gate_part, out_part, in_norm_part, out_norm_part), (...  37.9 us
    all_to_all x1, blocking collectives, shards(): lax.all_to_all(d_tri, 'dap', split_axis=0, concat_axis=2, tiled=True)  27.8 us
    all_to_all x1, blocking collectives, shards(): lax.all_to_all(product, 'dap', split_axis=2, concat_axis=0, tiled=True)  27.7 us
    all_to_all x1, waiting for transfers between devices, shards(): lax.all_to_all(left_act, 'dap', split_axis=0, concat_axis=2, tiled=True)  25.2 us
    all_to_all x1, waiting for transfers between devices, shards(): lax.all_to_all(right_act, 'dap', split_axis=0, concat_axis=2, tiled=True)  24.5 us
    all_to_all x1, waiting for transfers between devices, shards(): lax.all_to_all(back_l, 'dap', split_axis=2, concat_axis=0, tiled=True)  22.6 us
    unnamed x61, local copies, waits for them, and re-layouts  18.7 us
  transfers between devices with their start and end apart: 5, of which 5 were waited for; matrix products, arithmetic and copies ran while one was open for 4% of the time, Pallas kernels for 0%

commit v1 on v0

v1 whole, which is shorter than its diff:
```python
import functools

import jax
import jax.numpy as jnp
from jax import lax
from jax.experimental import pallas as pl
from jax.experimental.pallas import tpu as pltpu
from jax.sharding import PartitionSpec as P

epsilon = 1e-05
f32 = jnp.float32
bf16 = jnp.bfloat16
STEP = 4


def mm(a, b):
    return jnp.dot(a, b, preferred_element_type=f32)


def mm_t(a, b):
    return lax.dot_general(a, b, (((1,), (1,)), ((), ())), preferred_element_type=f32)


def sigmoid(v):
    return 0.5 * jnp.tanh(0.5 * v) + 0.5


def norm_cols(values):
    count = values.shape[0]
    centred = values - jnp.sum(values, axis=0, keepdims=True) * (1.0 / count)
    var = jnp.sum(centred * centred, axis=0, keepdims=True) * (1.0 / count)
    inv_std = lax.rsqrt(var + epsilon)
    return centred * inv_std, inv_std


def norm_back(grad_hat, x_hat, inv_std):
    count = grad_hat.shape[0]
    first = jnp.sum(grad_hat, axis=0, keepdims=True) * (1.0 / count)
    second = jnp.sum(grad_hat * x_hat, axis=0, keepdims=True) * (1.0 / count)
    return (grad_hat - first - x_hat * second) * inv_std


def fold(values, width):
    total = values[:, 0:width]
    for at in range(width, values.shape[1], width):
        total = total + values[:, at : at + width]
    return total


def kernel(
    groups,
    act,
    cot,
    in_gain,
    in_bias,
    w,
    w_t,
    wg,
    wg_t,
    out_gain,
    out_bias,
    wo,
    wo_t,
    eye,
    update,
    pair_grad,
    grads,
    act_all,
    cot_cols,
    left,
    right,
    tri_r,
    tri_c,
    col_act,
    col_cot,
    d_gate_sc,
    sums,
    recv_sem,
    right_sem,
    left_sem,
    cot_send,
    cot_recv,
):
    me = lax.axis_index("dap")
    rows, length, channels = act.shape
    hidden = wo.shape[0]

    barrier = pltpu.get_barrier_semaphore()
    for d in range(1, groups):
        pl.semaphore_signal(
            barrier,
            inc=1,
            device_id={"dap": lax.rem(me + d, groups)},
            device_id_type=pl.DeviceIdType.MESH,
        )
    pl.semaphore_wait(barrier, groups - 1)

    def hop(src, block, send_sems, to):
        return pltpu.make_async_remote_copy(
            src_ref=src,
            dst_ref=act_all.at[block],
            send_sem=send_sems.at[block],
            recv_sem=recv_sem.at[block],
            device_id={"dap": to},
            device_id_type=pl.DeviceIdType.MESH,
        )

    def cot_copy(d):
        peer = lax.rem(me + d, groups)
        at = pl.multiple_of(peer * rows, rows)
        mine = pl.multiple_of(me * rows, rows)
        return pltpu.make_async_remote_copy(
            src_ref=cot.at[:, pl.ds(at, rows), :],
            dst_ref=cot_cols.at[pl.ds(mine, rows)],
            send_sem=cot_send.at[d - 1],
            recv_sem=cot_recv.at[d - 1],
            device_id={"dap": peer},
            device_id_type=pl.DeviceIdType.MESH,
        )

    @pl.when(me + 1 < groups)
    def _():
        hop(act, me, right_sem, me + 1).start()

    @pl.when(me >= 1)
    def _():
        hop(act, me, left_sem, me - 1).start()

    for d in range(1, groups):
        cot_copy(d).start()

    def normed_of(x):
        hat, inv = norm_cols(mm_t(eye[...], x))
        return hat, inv, (hat * in_gain[...] + in_bias[...]).astype(bf16)

    def sides(src, base):
        def body(t, carry):
            x = src[pl.ds(t * STEP, STEP)].reshape(STEP * length, channels)
            _, _, normed = normed_of(x)
            pj = mm(w_t[...], normed)
            lv = sigmoid(pj[0:hidden]) * pj[hidden : 2 * hidden]
            rv = sigmoid(pj[2 * hidden : 3 * hidden]) * pj[3 * hidden : 4 * hidden]
            for r in range(STEP):
                row = base + t * STEP + r
                lanes = slice(r * length, (r + 1) * length)
                left[pl.ds(row, hidden, stride=length), :] = lv[:, lanes]
                right[pl.ds(row, hidden, stride=length), :] = rv[:, lanes]
                own = src[t * STEP + r, pl.ds(pl.multiple_of(me * rows, rows), rows), :]
                col_act[pl.ds(pl.multiple_of(row * rows, rows), rows), :] = own.astype(f32)
            return carry

        lax.fori_loop(0, rows // STEP, body, 0)

    sides(act, me * rows)
    for s in range(1, groups):
        low, high = me - s, me + s

        @pl.when(low >= 0)
        def _():
            hop(act, low, right_sem, me).wait_recv()

            @pl.when(me + 1 < groups)
            def _():
                hop(act_all.at[low], low, right_sem, me + 1).start()

        @pl.when(high < groups)
        def _():
            hop(act, high, left_sem, me).wait_recv()

            @pl.when(me >= 1)
            def _():
                hop(act_all.at[high], high, left_sem, me - 1).start()

        @pl.when(low >= 0)
        def _():
            sides(act_all.at[low], low * rows)

        @pl.when(high < groups)
        def _():
            sides(act_all.at[high], high * rows)

    mine = pl.multiple_of(me * rows, rows)

    def products(h, carry):
        at = pl.multiple_of(h * length, length)
        l_all = left[pl.ds(at, length), :].astype(bf16)
        r_all = right[pl.ds(at, length), :].astype(bf16)
        l_own = left[pl.ds(pl.multiple_of(at + mine, rows), rows), :].astype(bf16)
        r_own = right[pl.ds(pl.multiple_of(at + mine, rows), rows), :].astype(bf16)
        to = pl.ds(pl.multiple_of(h * rows, rows), rows)
        tri_r[to, :] = mm_t(l_own, r_all)
        tri_c[to, :] = mm_t(r_own, l_all)
        return carry

    lax.fori_loop(0, hidden, products, 0, unroll=4)

    def slabs(ref, first):
        return jnp.concatenate(
            [ref[pl.ds(first + r, hidden, stride=rows), :] for r in range(STEP)], axis=1
        )

    def put_slabs(ref, first, values):
        for r in range(STEP):
            ref[pl.ds(first + r, hidden, stride=rows), :] = values[
                :, r * length : (r + 1) * length
            ]

    sums[...] = jnp.zeros_like(sums)
    grads[...] = jnp.zeros_like(grads)
    pw = 4 * hidden

    def row_pass(t, carry):
        first = t * STEP
        x = act[pl.ds(first, STEP)].reshape(STEP * length, channels)
        _, _, normed = normed_of(x)
        gate = sigmoid(mm(wg_t[...], normed))
        hat, inv = norm_cols(slabs(tri_r, first).astype(bf16).astype(f32))
        tri_norm = (hat * out_gain[...] + out_bias[...]).astype(bf16)
        mixed = mm(wo_t[...], tri_norm)
        upd = (gate * mixed).astype(bf16)
        for r in range(STEP):
            update[first + r] = mm_t(eye[...], upd[:, r * length : (r + 1) * length]).astype(bf16)
        cot_t = mm_t(eye[...], cot[pl.ds(first, STEP)].reshape(STEP * length, channels))
        d_mixed_f = cot_t * gate
        d_mixed = d_mixed_f.astype(bf16)
        d_gate = (d_mixed_f * mixed * (1.0 - gate)).astype(bf16)
        d_gate_sc[t] = d_gate
        grads[:, pw : pw + channels] += mm_t(normed, d_gate)
        grads[:, pw + channels : pw + 2 * channels] += mm_t(tri_norm, d_mixed)
        d_out = mm(wo[...], d_mixed)
        sums[2] += fold(d_out * hat, length)
        sums[3] += fold(d_out, length)
        put_slabs(tri_r, first, norm_back(d_out * out_gain[...], hat, inv))
        return carry

    lax.fori_loop(0, rows // STEP, row_pass, 0)

    for d in range(1, groups):
        cot_copy(d).wait_recv()

    def unpack(t, carry):
        to = pl.ds(pl.multiple_of(t * rows, rows), rows)
        col_cot[to, :] = cot_cols[t].astype(f32)
        return carry

    def unpack_own(t, carry):
        to = pl.ds(pl.multiple_of((mine + t) * rows, rows), rows)
        col_cot[to, :] = cot[t, pl.ds(mine, rows), :].astype(f32)
        return carry

    for d in range(1, groups):
        peer = lax.rem(me + d, groups)
        lax.fori_loop(peer * rows, peer * rows + rows, unpack, 0)
    lax.fori_loop(0, rows, unpack_own, 0)

    def columns_of(ref, first):
        return jnp.concatenate(
            [ref[pl.ds(first + r, length, stride=rows), :] for r in range(STEP)], axis=0
        ).astype(bf16)

    def col_pass(t, carry):
        first = t * STEP
        _, _, normed = normed_of(columns_of(col_act, first))
        gate = sigmoid(mm(wg_t[...], normed))
        hat, inv = norm_cols(slabs(tri_c, first).astype(bf16).astype(f32))
        cot_t = mm_t(eye[...], columns_of(col_cot, first))
        d_out = mm(wo[...], (cot_t * gate).astype(bf16))
        put_slabs(tri_c, first, norm_back(d_out * out_gain[...], hat, inv))
        return carry

    lax.fori_loop(0, rows // STEP, col_pass, 0)

    def back_products(h, carry):
        at = pl.multiple_of(h * length, length)
        l_all = left[pl.ds(at, length), :].astype(bf16)
        r_all = right[pl.ds(at, length), :].astype(bf16)
        to = pl.ds(pl.multiple_of(h * rows, rows), rows)
        tri_r[to, :] = mm(tri_r[to, :].astype(bf16), r_all)
        tri_c[to, :] = mm(tri_c[to, :].astype(bf16), l_all)
        return carry

    lax.fori_loop(0, hidden, back_products, 0, unroll=4)

    def last_pass(t, carry):
        first = t * STEP
        x = act[pl.ds(first, STEP)].reshape(STEP * length, channels)
        hat, inv, normed = normed_of(x)
        pj = mm(w_t[...], normed)
        parts = []
        for side, ref in ((0, tri_r), (1, tri_c)):
            grad = slabs(ref, first).astype(bf16).astype(f32)
            sg = sigmoid(pj[2 * side * hidden : (2 * side + 1) * hidden])
            val = pj[(2 * side + 1) * hidden : (2 * side + 2) * hidden]
            d_val = grad * sg
            parts.append((d_val * val * (1.0 - sg)).astype(bf16))
            parts.append(d_val.astype(bf16))
        d_proj = jnp.concatenate(parts, axis=0)
        grads[:, 0:pw] += mm_t(normed, d_proj)
        d_normed = mm(w[...], d_proj) + mm(wg[...], d_gate_sc[t])
        sums[0] += fold(d_normed * hat, length)
        sums[1] += fold(d_normed, length)
        back = norm_back(d_normed * in_gain[...], hat, inv).astype(bf16)
        for r in range(STEP):
            pair_grad[first + r] = mm_t(eye[...], back[:, r * length : (r + 1) * length]).astype(
                bf16
            )
        return carry

    lax.fori_loop(0, rows // STEP, last_pass, 0)

    for n in range(4):
        at = pw + 2 * channels + n * 8
        grads[:, at : at + 8] = jnp.broadcast_to(
            jnp.sum(sums[n], axis=1, keepdims=True), (channels, 8)
        )

    for s in range(groups):
        low, high = me - s, me + s

        @pl.when((low >= 0) & (me + 1 < groups))
        def _():
            hop(act, low, right_sem, me + 1).wait_send()

        @pl.when((high < groups) & (me >= 1))
        def _():
            hop(act, high, left_sem, me - 1).wait_send()

    for d in range(1, groups):
        cot_copy(d).wait_send()


def shards(
    groups,
    pair_act,
    pair_cot,
    in_gain,
    in_bias,
    proj_weight,
    gate_weight,
    out_gain,
    out_bias,
    out_weight,
):
    _, rows, length, channels = pair_act.shape
    hidden = out_weight.shape[0]
    act = pair_act.reshape(rows, length, channels)
    cot = pair_cot.reshape(rows, length, channels)
    width = 4 * hidden + 3 * channels
    vmem = pl.BlockSpec(memory_space=pltpu.VMEM)
    dma = pltpu.SemaphoreType.DMA
    update, pair_grad, grads = pl.pallas_call(
        functools.partial(kernel, groups),
        out_shape=(
            jax.ShapeDtypeStruct(act.shape, bf16),
            jax.ShapeDtypeStruct(act.shape, bf16),
            jax.ShapeDtypeStruct((channels, width), f32),
        ),
        in_specs=[vmem] * 13,
        out_specs=(vmem,) * 3,
        scratch_shapes=[
            pltpu.VMEM((groups, rows, length, channels), bf16),
            pltpu.VMEM((length, rows, channels), bf16),
            pltpu.VMEM((hidden * length, length), f32),
            pltpu.VMEM((hidden * length, length), f32),
            pltpu.VMEM((hidden * rows, length), f32),
            pltpu.VMEM((hidden * rows, length), f32),
            pltpu.VMEM((length * rows, channels), f32),
            pltpu.VMEM((length * rows, channels), f32),
            pltpu.VMEM((rows // STEP, channels, STEP * length), bf16),
            pltpu.VMEM((4, channels, length), f32),
            dma((groups,)),
            dma((groups,)),
            dma((groups,)),
            dma((groups - 1,)),
            dma((groups - 1,)),
        ],
        compiler_params=pltpu.CompilerParams(
            collective_id=0, has_side_effects=True, vmem_limit_bytes=60 * 1024 * 1024
        ),
        name="tri",
    )(
        act,
        cot,
        in_gain.reshape(channels, 1),
        in_bias.reshape(channels, 1),
        proj_weight,
        proj_weight.T,
        gate_weight,
        gate_weight.T,
        out_gain.reshape(hidden, 1),
        out_bias.reshape(hidden, 1),
        out_weight,
        out_weight.T,
        jnp.eye(channels, dtype=bf16),
    )
    total = lax.psum(grads, ("dp", "dap")) * (1.0 / length)
    a = 4 * hidden
    b = a + channels
    c = b + channels
    stats = total[:, c : c + 32 : 8].T
    return (
        update.reshape(pair_act.shape),
        pair_grad.reshape(pair_act.shape),
        total[:, 0:a],
        total[:, a:b],
        total[:, b:c],
        stats[0:2],
        stats[2:4],
    )


def solution(mesh):
    placed = (P("dp", "dap", None, None),) * 2 + (P(),) * 7
    return jax.shard_map(
        functools.partial(shards, mesh.shape["dap"]),
        mesh=mesh,
        in_specs=placed,
        out_specs=(P("dp", "dap", None, None), P("dp", "dap", None, None), P(), P(), P(), P(), P()),
        check_vma=False,
    )
```

time: 385 us -> 311 us (0.81)
  Pallas kernels: 0 us -> 153 us
  blocking collectives: 93.5 us -> 0 us
  waiting for transfers between devices: 178 us -> 127 us
  other arithmetic: 25.3 us -> 1.68 us
  matrix products: 20.1 us -> 0 us
  starting transfers between devices: 19.4 us -> 0.04 us
  local copies, waits for them, and re-layouts: 32.7 us -> 14.2 us
    pallas_call x0 -> x1, Pallas kernels: none -> 153 us  [shards(): pl.pallas_call(functools.partial(kernel, groups), out_shape=(jax.ShapeDty...]
    all_to_all x4 -> x0, waiting for transfers between devices: 90.2 us -> none  [the longest x1 25.2 us: shards(): lax.all_to_all(left_act, 'dap', split_axis=0, concat_axis=2, tiled=True)]
    all_to_all x2 -> x0, blocking collectives: 55.5 us -> none  [the longest x1 27.8 us: shards(): lax.all_to_all(d_tri, 'dap', split_axis=0, concat_axis=2, tiled=True)]
    psum x1, waiting for transfers between devices: 88 us -> 127 us  [shards(): total = lax.psum(grads, ('dp', 'dap')) * (1.0 / length)]
    psum x1 -> x0, blocking collectives: 37.9 us -> none  [shards(): lax.psum((proj_part, gate_part, out_part, in_norm_part, out_norm_part), (...]
    dot_general x12 -> x0, matrix products: 20.1 us -> none  [the longest x1 2.95 us: shards(): jnp.einsum('hm,ch->mc', d_proj, proj_weight, preferred_element_type=f32)]
    all_to_all x4 -> x0, starting transfers between devices: 19.4 us -> none  [the longest x1 6.35 us: shards(): lax.all_to_all(right_act, 'dap', split_axis=0, concat_axis=2, tiled=True)]
    convert_element_type x8 -> x0, local copies, waits for them, and re-layouts: 12.4 us -> none  [the longest x1 2.92 us: shards(): left_grad = d_left.reshape(hidden_w, cell_count).astype(f32)]
  transfers between devices with their start and end apart: 5 -> 1, of which waited for: 5 -> 1; matrix products, arithmetic and copies ran while one was open for 4% -> 0% of each run, Pallas kernels for 0% -> 0%
where the time goes in v1:
time: 311 us; the launch traced here: 310 us
  Pallas kernels  153 us (49%)
  waiting for transfers between devices  127 us (41%)
  local copies, waits for them, and re-layouts  14.2 us (5%)
  between operations  14.1 us (5%)
    pallas_call x1, Pallas kernels, shards(): pl.pallas_call(functools.partial(kernel, groups), out_shape=(jax.ShapeDty...  153 us
    psum x1, waiting for transfers between devices, shards(): total = lax.psum(grads, ('dp', 'dap')) * (1.0 / length)  127 us
    unnamed x23, local copies, waits for them, and re-layouts  9.62 us
  transfers between devices with their start and end apart: 1, of which 1 were waited for; matrix products, arithmetic and copies ran while one was open for 0% of the time, Pallas kernels for 0%

profile of v1, /device:TPU:0, one launch (start us, length us, event | category | flops | bytes accessed | tf_op | source)
XLA Modules:
  0.0 310.3 jit_solution(4704354648623843462)
XLA Ops:
  7.2 0.0 all-reduce.2.cloned.1.call-start
  7.2 0.6 fusion.eye
  7.8 1.7 copy.16
  9.5 0.0 copy-start.4
  9.5 0.7 copy-done.4
  10.2 0.7 copy.19.in_gain
  10.9 0.0 copy-start.5
  10.9 0.7 copy-done.5
  11.6 0.7 copy.20.in_bias
  12.3 0.0 copy-start.6
  12.3 0.7 copy-done.6
  13.0 0.7 copy.21.out_gain
  13.7 0.0 copy-start.7
  13.7 0.7 copy-done.7
  14.3 0.0 copy-start.2
  14.3 0.7 copy.22.out_bias
  15.1 0.0 copy-done.2
  15.1 0.0 copy-start.3
  15.1 0.7 copy.17
  15.8 0.0 copy-done.3
  15.9 0.7 copy.18
  16.6 153.0 %tri.1 = (bf16[32,128,128]{2,1,0:T(8,128)(2,1)}, bf16[32,128,128]{2,1,0:T(8,128)(2,1)}, f32[128,896]{1,0:T(8,128)}) custom-call(bf16[32,128,128]{2,1,0:T(8,128)(2,1)} %bitcast.12, bf16[32,128,128]{2,1,0:T(8,128)(2,1)} %bitcast.13, f32[128,1]{1,0:T(8,128)} %copy.19.in_gain, f32[128,1]{1,0:T(8,128)} %copy.20.in_bias, bf16[128,512]{1,0:T(8,128)(2,1)} %w.1, ...), custom_call_target="tpu_custom_call" | custom-call | tf_op jit(solution)/shard_map/tri/pallas_call | solution.py:351
  169.6 0.0 all-reduce.2.cloned.1.call-update
  169.6 0.0 copy-start.1
  169.6 127.3 %all-reduce.2.cloned.1.call-done = f32[128,896]{1,0:T(8,128)} async-done(((f32[128,896]{1,0:T(8,128)}), f32[128,896]{1,0:T(8,128)}) %all-reduce.2.cloned.1.call-update) | async-done | bytes 458768 | tf_op jit(solution)/shard_map/psum | solution.py:396
  297.0 1.0 broadcast_multiply_fusion
  298.0 0.1 slice.21
  298.1 0.7 fusion.1
  298.8 0.7 slice.24
  299.5 0.1 fusion.2
  299.6 0.6 copy.23
  300.2 0.6 copy.24
  300.9 0.0 copy-done.1
  300.9 0.0 copy-start
  300.9 1.0 copy.28
  301.9 0.6 copy-done
  302.5 1.0 copy.29
Async XLA Ops:
  7.2 289.8 %all-reduce.2.cloned.1.call-start = ((), (), s32[]{:S(2)}) async-start(), calls=%async_computation | async-start | bytes 917504 | tf_op jit(solution)/shard_map/psum | solution.py:396
  9.5 0.7 copy-start.4
  10.9 0.7 copy-start.5
  12.3 0.7 copy-start.6
  13.7 0.7 copy-start.7
  14.3 0.8 copy-start.2
  15.1 0.8 copy-start.3
  169.6 131.2 %copy-start.1 = (bf16[32,128,128]{2,1,0:T(8,128)(2,1)S(1)}, bf16[32,128,128]{2,1,0:T(8,128)(2,1)}, u32[]{:S(2)}) copy-start(bf16[32,128,128]{2,1,0:T(8,128)(2,1)} %get-tuple-element.10) | copy-start | bytes 3145732
  300.9 1.6 copy-start
Sparse Core Ops, SparseCore 0:
  169.8 127.1 all-reduce.1

commit v2 on v1

--- a/solution.py
+++ b/solution.py
@@ -48,23 +48,24 @@
 
 
 def kernel(
+    crops,
     groups,
     act,
     cot,
-    in_gain,
-    in_bias,
+    in_gain_row,
+    in_bias_row,
     w,
-    w_t,
     wg,
-    wg_t,
-    out_gain,
-    out_bias,
+    out_gain_row,
+    out_bias_row,
     wo,
-    wo_t,
-    eye,
     update,
     pair_grad,
-    grads,
+    proj_grad,
+    gate_grad,
+    out_grad,
+    in_norm_grad,
+    out_norm_grad,
     act_all,
     cot_cols,
     left,
@@ -80,8 +81,20 @@
     left_sem,
     cot_send,
     cot_recv,
+    w_t,
+    wg_t,
+    wo_t,
+    eye,
+    columns,
+    early,
+    late,
+    early_bufs,
+    late_bufs,
+    sum_sems,
+    swap_sems,
 ):
     me = lax.axis_index("dap")
+    crop = lax.axis_index("dp")
     rows, length, channels = act.shape
     hidden = wo.shape[0]
 
@@ -93,7 +106,14 @@
             device_id={"dap": lax.rem(me + d, groups)},
             device_id_type=pl.DeviceIdType.MESH,
         )
-    pl.semaphore_wait(barrier, groups - 1)
+    for d in range(1, crops):
+        pl.semaphore_signal(
+            barrier,
+            inc=1,
+            device_id={"dp": lax.rem(crop + d, crops)},
+            device_id_type=pl.DeviceIdType.MESH,
+        )
+    pl.semaphore_wait(barrier, groups + crops - 2)
 
     def hop(src, block, send_sems, to):
         return pltpu.make_async_remote_copy(
@@ -128,6 +148,98 @@
 
     for d in range(1, groups):
         cot_copy(d).start()
+
+    def turned(block):
+        return jnp.transpose(block.astype(f32)).astype(bf16)
+
+    for n in range(4):
+        w_t[n * hidden : (n + 1) * hidden, :] = turned(w[:, n * hidden : (n + 1) * hidden])
+    wg_t[...] = turned(wg[...])
+    wo_t[...] = turned(wo[...])
+    square = (channels, channels)
+    eye[...] = (
+        (lax.broadcasted_iota(jnp.int32, square, 0) == lax.broadcasted_iota(jnp.int32, square, 1))
+        .astype(f32)
+        .astype(bf16)
+    )
+    for n, row in enumerate((in_gain_row, in_bias_row, out_gain_row, out_bias_row)):
+        columns[n] = jnp.transpose(jnp.broadcast_to(row[...], square))[:, 0:1]
+    in_gain, in_bias, out_gain, out_bias = (columns.at[n] for n in range(4))
+
+    def piece_copy(which, stage, bufs, e):
+        peer = lax.rem(crop + e, crops)
+        sent, got, _, total = bufs
+        src, dst = (sent.at[peer], got.at[crop]) if stage == 0 else (total.at[crop],) * 2
+        return pltpu.make_async_remote_copy(
+            src_ref=src,
+            dst_ref=dst,
+            send_sem=sum_sems.at[which, stage, 0, e - 1],
+            recv_sem=sum_sems.at[which, stage, 1, e - 1],
+            device_id={"dp": peer},
+            device_id_type=pl.DeviceIdType.MESH,
+        )
+
+    def swap_copy(which, bufs, d):
+        part = bufs[2]
+        return pltpu.make_async_remote_copy(
+            src_ref=part.at[me],
+            dst_ref=part.at[me],
+            send_sem=swap_sems.at[which, 0, d - 1],
+            recv_sem=swap_sems.at[which, 1, d - 1],
+            device_id={"dap": lax.rem(me + d, groups)},
+            device_id_type=pl.DeviceIdType.MESH,
+        )
+
+    piece = channels // crops
+
+    def sum_first(which, acc, bufs):
+        for p in range(crops):
+            bufs[0][p] = acc[p * piece : (p + 1) * piece, :]
+        for e in range(1, crops):
+            piece_copy(which, 0, bufs, e).start()
+
+    def sum_second(which, bufs):
+        total = bufs[0][crop]
+        for e in range(1, crops):
+            piece_copy(which, 0, bufs, e).wait_recv()
+            total = total + bufs[1][lax.rem(crop + crops - e, crops)]
+        bufs[2][me] = total
+        for d in range(1, groups):
+            swap_copy(which, bufs, d).start()
+
+    def sum_third(which, bufs):
+        for d in range(1, groups):
+            swap_copy(which, bufs, d).wait_recv()
+        total = bufs[2][0]
+        for g in range(1, groups):
+            total = total + bufs[2][g]
+        bufs[3][crop] = total * (1.0 / length)
+        for e in range(1, crops):
+            piece_copy(which, 1, bufs, e).start()
+
+    def sum_last(which, bufs, outs, stats_out):
+        for e in range(1, crops):
+            piece_copy(which, 1, bufs, e).wait_recv()
+        total = jnp.concatenate([bufs[3][p] for p in range(crops)], axis=0)
+        at = 0
+        for out in outs:
+            out[...] = total[:, at : at + out.shape[1]]
+            at += out.shape[1]
+        turned_stats = jnp.transpose(total[:, at : at + channels])
+        stats_out[0:1, :] = turned_stats[0:1]
+        stats_out[1:2, :] = turned_stats[8:9]
+        for e in range(1, crops):
+            piece_copy(which, 0, bufs, e).wait_send()
+            piece_copy(which, 1, bufs, e).wait_send()
+        for d in range(1, groups):
+            swap_copy(which, bufs, d).wait_send()
+
+    def put_stats(acc, first):
+        at = acc.shape[1] - channels
+        for n in range(2):
+            acc[:, at + 8 * n : at + 8 * n + 8] = jnp.broadcast_to(
+                jnp.sum(sums[first + n], axis=1, keepdims=True), (channels, 8)
+            )
 
     def normed_of(x):
         hat, inv = norm_cols(mm_t(eye[...], x))
@@ -206,7 +318,8 @@
             ]
 
     sums[...] = jnp.zeros_like(sums)
-    grads[...] = jnp.zeros_like(grads)
+    early[...] = jnp.zeros_like(early)
+    late[...] = jnp.zeros_like(late)
     pw = 4 * hidden
 
     def row_pass(t, carry):
@@ -225,8 +338,8 @@
         d_mixed = d_mixed_f.astype(bf16)
         d_gate = (d_mixed_f * mixed * (1.0 - gate)).astype(bf16)
         d_gate_sc[t] = d_gate
-        grads[:, pw : pw + channels] += mm_t(normed, d_gate)
-        grads[:, pw + channels : pw + 2 * channels] += mm_t(tri_norm, d_mixed)
+        early[:, 0:channels] += mm_t(normed, d_gate)
+        early[:, channels : 2 * channels] += mm_t(tri_norm, d_mixed)
         d_out = mm(wo[...], d_mixed)
         sums[2] += fold(d_out * hat, length)
         sums[3] += fold(d_out, length)
@@ -234,6 +347,8 @@
         return carry
 
     lax.fori_loop(0, rows // STEP, row_pass, 0)
+    put_stats(early, 2)
+    sum_first(0, early, early_bufs)
 
     for d in range(1, groups):
         cot_copy(d).wait_recv()
@@ -269,6 +384,7 @@
         return carry
 
     lax.fori_loop(0, rows // STEP, col_pass, 0)
+    sum_second(0, early_bufs)
 
     def back_products(h, carry):
         at = pl.multiple_of(h * length, length)
@@ -280,6 +396,7 @@
         return carry
 
     lax.fori_loop(0, hidden, back_products, 0, unroll=4)
+    sum_third(0, early_bufs)
 
     def last_pass(t, carry):
         first = t * STEP
@@ -295,7 +412,7 @@
             parts.append((d_val * val * (1.0 - sg)).astype(bf16))
             parts.append(d_val.astype(bf16))
         d_proj = jnp.concatenate(parts, axis=0)
-        grads[:, 0:pw] += mm_t(normed, d_proj)
+        late[:, 0:pw] += mm_t(normed, d_proj)
         d_normed = mm(w[...], d_proj) + mm(wg[...], d_gate_sc[t])
         sums[0] += fold(d_normed * hat, length)
         sums[1] += fold(d_normed, length)
@@ -308,11 +425,12 @@
 
     lax.fori_loop(0, rows // STEP, last_pass, 0)
 
-    for n in range(4):
-        at = pw + 2 * channels + n * 8
-        grads[:, at : at + 8] = jnp.broadcast_to(
-            jnp.sum(sums[n], axis=1, keepdims=True), (channels, 8)
-        )
+    put_stats(late, 0)
+    sum_first(1, late, late_bufs)
+    sum_last(0, early_bufs, (gate_grad, out_grad), out_norm_grad)
+    sum_second(1, late_bufs)
+    sum_third(1, late_bufs)
+    sum_last(1, late_bufs, (proj_grad,), in_norm_grad)
 
     for s in range(groups):
         low, high = me - s, me + s
@@ -330,6 +448,7 @@
 
 
 def shards(
+    crops,
     groups,
     pair_act,
     pair_cot,
@@ -345,18 +464,27 @@
     hidden = out_weight.shape[0]
     act = pair_act.reshape(rows, length, channels)
     cot = pair_cot.reshape(rows, length, channels)
-    width = 4 * hidden + 3 * channels
     vmem = pl.BlockSpec(memory_space=pltpu.VMEM)
     dma = pltpu.SemaphoreType.DMA
-    update, pair_grad, grads = pl.pallas_call(
-        functools.partial(kernel, groups),
+    piece = channels // crops
+
+    def sum_bufs(width):
+        return tuple(pltpu.VMEM((n, piece, width), f32) for n in (crops, crops, groups, crops))
+
+    early_width, late_width = 3 * channels, 4 * hidden + channels
+    update, pair_grad, *grads = pl.pallas_call(
+        functools.partial(kernel, crops, groups),
         out_shape=(
             jax.ShapeDtypeStruct(act.shape, bf16),
             jax.ShapeDtypeStruct(act.shape, bf16),
-            jax.ShapeDtypeStruct((channels, width), f32),
+            jax.ShapeDtypeStruct(proj_weight.shape, f32),
+            jax.ShapeDtypeStruct(gate_weight.shape, f32),
+            jax.ShapeDtypeStruct(out_weight.shape, f32),
+            jax.ShapeDtypeStruct((2, channels), f32),
+            jax.ShapeDtypeStruct((2, hidden), f32),
         ),
-        in_specs=[vmem] * 13,
-        out_specs=(vmem,) * 3,
+        in_specs=[vmem] * 9,
+        out_specs=(vmem,) * 7,
         scratch_shapes=[
             pltpu.VMEM((groups, rows, length, channels), bf16),
             pltpu.VMEM((length, rows, channels), bf16),
@@ -373,6 +501,17 @@
             dma((groups,)),
             dma((groups - 1,)),
             dma((groups - 1,)),
+            pltpu.VMEM((4 * hidden, channels), bf16),
+            pltpu.VMEM((channels, channels), bf16),
+            pltpu.VMEM((channels, hidden), bf16),
+            pltpu.VMEM((channels, channels), bf16),
+            pltpu.VMEM((4, channels, 1), f32),
+            pltpu.VMEM((channels, early_width), f32),
+            pltpu.VMEM((channels, late_width), f32),
+            sum_bufs(early_width),
+            sum_bufs(late_width),
+            dma((2, 2, 2, crops - 1)),
+            dma((2, 2, groups - 1)),
         ],
         compiler_params=pltpu.CompilerParams(
             collective_id=0, has_side_effects=True, vmem_limit_bytes=60 * 1024 * 1024
@@ -381,38 +520,21 @@
     )(
         act,
         cot,
-        in_gain.reshape(channels, 1),
-        in_bias.reshape(channels, 1),
+        in_gain.reshape(1, channels),
+        in_bias.reshape(1, channels),
         proj_weight,
-        proj_weight.T,
         gate_weight,
-        gate_weight.T,
-        out_gain.reshape(hidden, 1),
-        out_bias.reshape(hidden, 1),
+        out_gain.reshape(1, hidden),
+        out_bias.reshape(1, hidden),
         out_weight,
-        out_weight.T,
-        jnp.eye(channels, dtype=bf16),
     )
-    total = lax.psum(grads, ("dp", "dap")) * (1.0 / length)
-    a = 4 * hidden
-    b = a + channels
-    c = b + channels
-    stats = total[:, c : c + 32 : 8].T
-    return (
-        update.reshape(pair_act.shape),
-        pair_grad.reshape(pair_act.shape),
-        total[:, 0:a],
-        total[:, a:b],
-        total[:, b:c],
-        stats[0:2],
-        stats[2:4],
-    )
+    return (update.reshape(pair_act.shape), pair_grad.reshape(pair_act.shape), *grads)
 
 
 def solution(mesh):
     placed = (P("dp", "dap", None, None),) * 2 + (P(),) * 7
     return jax.shard_map(
-        functools.partial(shards, mesh.shape["dap"]),
+        functools.partial(shards, mesh.shape["dp"], mesh.shape["dap"]),
         mesh=mesh,
         in_specs=placed,
         out_specs=(P("dp", "dap", None, None), P("dp", "dap", None, None), P(), P(), P(), P(), P()),

time: 311 us -> 176 us (0.57)
  waiting for transfers between devices: 127 us -> 0 us
  Pallas kernels: 153 us -> 167 us
  between operations: 14.1 us -> 0.66 us
  local copies, waits for them, and re-layouts: 14.2 us -> 7.11 us
    psum x1 -> x0, waiting for transfers between devices: 127 us -> none  [shards(): total = lax.psum(grads, ('dp', 'dap')) * (1.0 / length)]
    pallas_call x1, Pallas kernels: 153 us -> 167 us  [shards(): pl.pallas_call(functools.partial(kernel, crops, groups), out_shape=(jax.S...]
    unnamed x23 -> x19, local copies, waits for them, and re-layouts: 9.62 us -> 7.11 us
  transfers between devices with their start and end apart: 1 -> 0, of which waited for: 1 -> 0; matrix products, arithmetic and copies ran while one was open for 0% -> 0% of each run, Pallas kernels for 0% -> 0%
where the time goes in v2:
time: 176 us; the launch traced here: 175 us
  Pallas kernels  167 us (95%)
  local copies, waits for them, and re-layouts  7.11 us (4%)
    pallas_call x1, Pallas kernels, shards(): pl.pallas_call(functools.partial(kernel, crops, groups), out_shape=(jax.S...  167 us
    unnamed x19, local copies, waits for them, and re-layouts  7.11 us

profile of v2, /device:TPU:0, one launch (start us, length us, event | category | flops | bytes accessed | tf_op | source)
XLA Modules:
  0.0 175.2 jit_solution(18313466218054534020)
XLA Ops:
  0.6 167.5 %tri.1 = (bf16[32,128,128]{2,1,0:T(8,128)(2,1)}, bf16[32,128,128]{2,1,0:T(8,128)(2,1)}, f32[128,512]{1,0:T(8,128)}, f32[128,128]{1,0:T(8,128)}, f32[128,128]{1,0...) custom-call(bf16[32,128,128]{2,1,0:T(8,128)(2,1)} %bitcast.10, bf16[32,128,128]{2,1,0:T(8,128)(2,1)} %bitcast.11, ...), custom_call_target="tpu_custom_call" | custom-call | tf_op jit(solution)/shard_map/tri/pallas_call | solution.py:475
  168.1 0.0 copy-start
  168.1 2.4 %copy.23 = bf16[1,32,128,128]{3,2,1,0:T(8,128)(2,1)} copy(bf16[1,32,128,128]{3,2,1,0:T(8,128)(2,1)} %bitcast.9) | data formatting | bytes 2097152
  170.5 0.0 copy-done
  170.5 0.0 copy-start.1
  170.5 1.0 copy.24
  171.5 0.1 copy-done.1
  171.6 0.0 copy-start.3
  171.6 0.7 copy.25
  172.3 0.2 copy-done.3
  172.5 0.0 copy-start.2
  172.5 0.6 copy.26
  173.1 0.2 copy-done.2
  173.3 0.0 copy-start.5
  173.3 0.6 copy.27
  174.0 0.0 copy-done.5
  174.0 0.0 copy-start.4
  174.0 0.6 copy.28
  174.6 0.1 copy-done.4
  174.7 0.6 copy.29
Async XLA Ops:
  168.1 2.4 %copy-start = (bf16[32,128,128]{2,1,0:T(8,128)(2,1)S(1)}, bf16[32,128,128]{2,1,0:T(8,128)(2,1)}, u32[]{:S(2)}) copy-start(bf16[32,128,128]{2,1,0:T(8,128)(2,1)} %get-tuple-element.15) | copy-start | bytes 3145732
  170.5 1.1 copy-start.1
  171.6 0.9 copy-start.3
  172.5 0.9 copy-start.2
  173.3 0.7 copy-start.5
  174.0 0.7 copy-start.4

commit v3 on v2

--- a/solution.py
+++ b/solution.py
@@ -92,6 +92,7 @@
     late_bufs,
     sum_sems,
     swap_sems,
+    d_normed_sc,
 ):
     me = lax.axis_index("dap")
     crop = lax.axis_index("dp")
@@ -145,9 +146,6 @@
     @pl.when(me >= 1)
     def _():
         hop(act, me, left_sem, me - 1).start()
-
-    for d in range(1, groups):
-        cot_copy(d).start()
 
     def turned(block):
         return jnp.transpose(block.astype(f32)).astype(bf16)
@@ -283,6 +281,10 @@
             def _():
                 hop(act_all.at[high], high, left_sem, me - 1).start()
 
+        if s == groups - 1:
+            for d in range(1, groups):
+                cot_copy(d).start()
+
         @pl.when(low >= 0)
         def _():
             sides(act_all.at[low], low * rows)
@@ -320,7 +322,6 @@
     sums[...] = jnp.zeros_like(sums)
     early[...] = jnp.zeros_like(early)
     late[...] = jnp.zeros_like(late)
-    pw = 4 * hidden
 
     def row_pass(t, carry):
         first = t * STEP
@@ -347,11 +348,36 @@
         return carry
 
     lax.fori_loop(0, rows // STEP, row_pass, 0)
+
+    def back_rows(h, carry):
+        r_all = right[pl.ds(pl.multiple_of(h * length, length), length), :].astype(bf16)
+        to = pl.ds(pl.multiple_of(h * rows, rows), rows)
+        tri_r[to, :] = mm(tri_r[to, :].astype(bf16), r_all)
+        return carry
+
+    lax.fori_loop(0, hidden, back_rows, 0, unroll=8)
+
+    half = 2 * hidden
+
+    def half_grad(ref, first, pj):
+        grad = slabs(ref, first).astype(bf16).astype(f32)
+        sg = sigmoid(pj[0:hidden])
+        d_val = grad * sg
+        d_pre = d_val * pj[hidden:half] * (1.0 - sg)
+        return jnp.concatenate([d_pre.astype(bf16), d_val.astype(bf16)], axis=0)
+
+    def left_pass(t, carry):
+        first = t * STEP
+        x = act[pl.ds(first, STEP)].reshape(STEP * length, channels)
+        _, _, normed = normed_of(x)
+        d_proj = half_grad(tri_r, first, mm(w_t[0:half, :], normed))
+        early[:, 2 * channels : 2 * channels + half] += mm_t(normed, d_proj)
+        d_normed_sc[t] = mm(w[:, 0:half], d_proj) + mm(wg[...], d_gate_sc[t])
+        return carry
+
+    lax.fori_loop(0, rows // STEP, left_pass, 0)
     put_stats(early, 2)
     sum_first(0, early, early_bufs)
-
-    for d in range(1, groups):
-        cot_copy(d).wait_recv()
 
     def unpack(t, carry):
         to = pl.ds(pl.multiple_of(t * rows, rows), rows)
@@ -363,10 +389,12 @@
         col_cot[to, :] = cot[t, pl.ds(mine, rows), :].astype(f32)
         return carry
 
+    lax.fori_loop(0, rows, unpack_own, 0)
+    for d in range(1, groups):
+        cot_copy(d).wait_recv()
     for d in range(1, groups):
         peer = lax.rem(me + d, groups)
         lax.fori_loop(peer * rows, peer * rows + rows, unpack, 0)
-    lax.fori_loop(0, rows, unpack_own, 0)
 
     def columns_of(ref, first):
         return jnp.concatenate(
@@ -386,34 +414,22 @@
     lax.fori_loop(0, rows // STEP, col_pass, 0)
     sum_second(0, early_bufs)
 
-    def back_products(h, carry):
-        at = pl.multiple_of(h * length, length)
-        l_all = left[pl.ds(at, length), :].astype(bf16)
-        r_all = right[pl.ds(at, length), :].astype(bf16)
+    def back_cols(h, carry):
+        l_all = left[pl.ds(pl.multiple_of(h * length, length), length), :].astype(bf16)
         to = pl.ds(pl.multiple_of(h * rows, rows), rows)
-        tri_r[to, :] = mm(tri_r[to, :].astype(bf16), r_all)
         tri_c[to, :] = mm(tri_c[to, :].astype(bf16), l_all)
         return carry
 
-    lax.fori_loop(0, hidden, back_products, 0, unroll=4)
+    lax.fori_loop(0, hidden, back_cols, 0, unroll=8)
     sum_third(0, early_bufs)
 
     def last_pass(t, carry):
         first = t * STEP
         x = act[pl.ds(first, STEP)].reshape(STEP * length, channels)
         hat, inv, normed = normed_of(x)
-        pj = mm(w_t[...], normed)
-        parts = []
-        for side, ref in ((0, tri_r), (1, tri_c)):
-            grad = slabs(ref, first).astype(bf16).astype(f32)
-            sg = sigmoid(pj[2 * side * hidden : (2 * side + 1) * hidden])
-            val = pj[(2 * side + 1) * hidden : (2 * side + 2) * hidden]
-            d_val = grad * sg
-            parts.append((d_val * val * (1.0 - sg)).astype(bf16))
-            parts.append(d_val.astype(bf16))
-        d_proj = jnp.concatenate(parts, axis=0)
-        late[:, 0:pw] += mm_t(normed, d_proj)
-        d_normed = mm(w[...], d_proj) + mm(wg[...], d_gate_sc[t])
+        d_proj = half_grad(tri_c, first, mm(w_t[half : 2 * half, :], normed))
+        late[:, 0:half] += mm_t(normed, d_proj)
+        d_normed = mm(w[:, half : 2 * half], d_proj) + d_normed_sc[t]
         sums[0] += fold(d_normed * hat, length)
         sums[1] += fold(d_normed, length)
         back = norm_back(d_normed * in_gain[...], hat, inv).astype(bf16)
@@ -427,10 +443,10 @@
 
     put_stats(late, 0)
     sum_first(1, late, late_bufs)
-    sum_last(0, early_bufs, (gate_grad, out_grad), out_norm_grad)
+    sum_last(0, early_bufs, (gate_grad, out_grad, proj_grad.at[:, 0:half]), out_norm_grad)
     sum_second(1, late_bufs)
     sum_third(1, late_bufs)
-    sum_last(1, late_bufs, (proj_grad,), in_norm_grad)
+    sum_last(1, late_bufs, (proj_grad.at[:, half : 2 * half],), in_norm_grad)
 
     for s in range(groups):
         low, high = me - s, me + s
@@ -471,7 +487,7 @@
     def sum_bufs(width):
         return tuple(pltpu.VMEM((n, piece, width), f32) for n in (crops, crops, groups, crops))
 
-    early_width, late_width = 3 * channels, 4 * hidden + channels
+    early_width, late_width = 3 * channels + 2 * hidden, 2 * hidden + channels
     update, pair_grad, *grads = pl.pallas_call(
         functools.partial(kernel, crops, groups),
         out_shape=(
@@ -512,6 +528,7 @@
             sum_bufs(late_width),
             dma((2, 2, 2, crops - 1)),
             dma((2, 2, groups - 1)),
+            pltpu.VMEM((rows // STEP, channels, STEP * length), f32),
         ],
         compiler_params=pltpu.CompilerParams(
             collective_id=0, has_side_effects=True, vmem_limit_bytes=60 * 1024 * 1024

time: 176 us -> 170 us (0.966)
  Pallas kernels: 167 us -> 162 us
    pallas_call x1, Pallas kernels: 167 us -> 162 us  [shards(): pl.pallas_call(functools.partial(kernel, crops, groups), out_shape=(jax.S...]
where the time goes in v3:
time: 170 us
  Pallas kernels  162 us (95%)
  local copies, waits for them, and re-layouts  7.11 us (4%)
    pallas_call x1, Pallas kernels, shards(): pl.pallas_call(functools.partial(kernel, crops, groups), out_shape=(jax.S...  162 us
    unnamed x19, local copies, waits for them, and re-layouts  7.11 us

profile of v3, /device:TPU:0, one launch (start us, length us, event | category | flops | bytes accessed | tf_op | source)
XLA Modules:
  0.0 170.0 jit_solution(1864081824766491517)
XLA Ops:
  0.6 162.2 %tri.1 = (bf16[32,128,128]{2,1,0:T(8,128)(2,1)}, bf16[32,128,128]{2,1,0:T(8,128)(2,1)}, f32[128,512]{1,0:T(8,128)}, f32[128,128]{1,0:T(8,128)}, f32[128,128]{1,0...) custom-call(bf16[32,128,128]{2,1,0:T(8,128)(2,1)} %bitcast.10, bf16[32,128,128]{2,1,0:T(8,128)(2,1)} %bitcast.11, ...), custom_call_target="tpu_custom_call" | custom-call | tf_op jit(solution)/shard_map/tri/pallas_call | solution.py:491
  162.9 0.0 copy-start
  162.9 2.4 %copy.23 = bf16[1,32,128,128]{3,2,1,0:T(8,128)(2,1)} copy(bf16[1,32,128,128]{3,2,1,0:T(8,128)(2,1)} %bitcast.9) | data formatting | bytes 2097152
  165.3 0.0 copy-done
  165.3 0.0 copy-start.1
  165.3 1.0 copy.24
  166.3 0.1 copy-done.1
  166.4 0.0 copy-start.3
  166.4 0.7 copy.25
  167.1 0.2 copy-done.3
  167.3 0.0 copy-start.2
  167.3 0.6 copy.26
  167.9 0.2 copy-done.2
  168.1 0.0 copy-start.5
  168.1 0.6 copy.27
  168.8 0.0 copy-done.5
  168.8 0.0 copy-start.4
  168.8 0.6 copy.28
  169.4 0.1 copy-done.4
  169.5 0.6 copy.29
Async XLA Ops:
  162.9 2.4 %copy-start = (bf16[32,128,128]{2,1,0:T(8,128)(2,1)S(1)}, bf16[32,128,128]{2,1,0:T(8,128)(2,1)}, u32[]{:S(2)}) copy-start(bf16[32,128,128]{2,1,0:T(8,128)(2,1)} %get-tuple-element.15) | copy-start | bytes 3145732
  165.3 1.1 copy-start.1
  166.4 0.9 copy-start.3
  167.3 0.9 copy-start.2
  168.1 0.7 copy-start.5
  168.8 0.7 copy-start.4

commit v4 on v3

--- a/solution.py
+++ b/solution.py
@@ -10,7 +10,8 @@
 epsilon = 1e-05
 f32 = jnp.float32
 bf16 = jnp.bfloat16
-STEP = 4
+STEP = 8
+CUTS = 2
 
 
 def mm(a, b):
@@ -116,12 +117,15 @@
         )
     pl.semaphore_wait(barrier, groups + crops - 2)
 
-    def hop(src, block, send_sems, to):
+    cut = rows // CUTS
+
+    def hop(src, block, c, send_sems, to):
+        part = pl.ds(c * cut, cut)
         return pltpu.make_async_remote_copy(
-            src_ref=src,
-            dst_ref=act_all.at[block],
-            send_sem=send_sems.at[block],
-            recv_sem=recv_sem.at[block],
+            src_ref=src.at[part],
+            dst_ref=act_all.at[block, part],
+            send_sem=send_sems.at[block, c],
+            recv_sem=recv_sem.at[block, c],
             device_id={"dap": to},
             device_id_type=pl.DeviceIdType.MESH,
         )
@@ -141,11 +145,13 @@
 
     @pl.when(me + 1 < groups)
     def _():
-        hop(act, me, right_sem, me + 1).start()
+        for c in range(CUTS):
+            hop(act, me, c, right_sem, me + 1).start()
 
     @pl.when(me >= 1)
     def _():
-        hop(act, me, left_sem, me - 1).start()
+        for c in range(CUTS):
+            hop(act, me, c, left_sem, me - 1).start()
 
     def turned(block):
         return jnp.transpose(block.astype(f32)).astype(bf16)
@@ -243,7 +249,7 @@
         hat, inv = norm_cols(mm_t(eye[...], x))
         return hat, inv, (hat * in_gain[...] + in_bias[...]).astype(bf16)
 
-    def sides(src, base):
+    def sides(src, base, start, count):
         def body(t, carry):
             x = src[pl.ds(t * STEP, STEP)].reshape(STEP * length, channels)
             _, _, normed = normed_of(x)
@@ -259,39 +265,40 @@
                 col_act[pl.ds(pl.multiple_of(row * rows, rows), rows), :] = own.astype(f32)
             return carry
 
-        lax.fori_loop(0, rows // STEP, body, 0)
-
-    sides(act, me * rows)
+        lax.fori_loop(start // STEP, (start + count) // STEP, body, 0)
+
+    sides(act, me * rows, 0, rows)
     for s in range(1, groups):
         low, high = me - s, me + s
-
-        @pl.when(low >= 0)
-        def _():
-            hop(act, low, right_sem, me).wait_recv()
-
-            @pl.when(me + 1 < groups)
+        for c in range(CUTS):
+
+            @pl.when(low >= 0)
             def _():
-                hop(act_all.at[low], low, right_sem, me + 1).start()
-
-        @pl.when(high < groups)
-        def _():
-            hop(act, high, left_sem, me).wait_recv()
-
-            @pl.when(me >= 1)
+                hop(act, low, c, right_sem, me).wait_recv()
+
+                @pl.when(me + 1 < groups)
+                def _():
+                    hop(act_all.at[low], low, c, right_sem, me + 1).start()
+
+            @pl.when(high < groups)
             def _():
-                hop(act_all.at[high], high, left_sem, me - 1).start()
-
-        if s == groups - 1:
-            for d in range(1, groups):
-                cot_copy(d).start()
-
-        @pl.when(low >= 0)
-        def _():
-            sides(act_all.at[low], low * rows)
-
-        @pl.when(high < groups)
-        def _():
-            sides(act_all.at[high], high * rows)
+                hop(act, high, c, left_sem, me).wait_recv()
+
+                @pl.when(me >= 1)
+                def _():
+                    hop(act_all.at[high], high, c, left_sem, me - 1).start()
+
+            if s == groups - 1 and c == CUTS - 1:
+                for d in range(1, groups):
+                    cot_copy(d).start()
+
+            @pl.when(low >= 0)
+            def _():
+                sides(act_all.at[low], low * rows, c * cut, cut)
+
+            @pl.when(high < groups)
+            def _():
+                sides(act_all.at[high], high * rows, c * cut, cut)
 
     mine = pl.multiple_of(me * rows, rows)
 
@@ -453,11 +460,13 @@
 
         @pl.when((low >= 0) & (me + 1 < groups))
         def _():
-            hop(act, low, right_sem, me + 1).wait_send()
+            for c in range(CUTS):
+                hop(act, low, c, right_sem, me + 1).wait_send()
 
         @pl.when((high < groups) & (me >= 1))
         def _():
-            hop(act, high, left_sem, me - 1).wait_send()
+            for c in range(CUTS):
+                hop(act, high, c, left_sem, me - 1).wait_send()
 
     for d in range(1, groups):
         cot_copy(d).wait_send()
@@ -512,9 +521,9 @@
             pltpu.VMEM((length * rows, channels), f32),
             pltpu.VMEM((rows // STEP, channels, STEP * length), bf16),
             pltpu.VMEM((4, channels, length), f32),
-            dma((groups,)),
-            dma((groups,)),
-            dma((groups,)),
+            dma((groups, CUTS)),
+            dma((groups, CUTS)),
+            dma((groups, CUTS)),
             dma((groups - 1,)),
             dma((groups - 1,)),
             pltpu.VMEM((4 * hidden, channels), bf16),

time: 170 us -> 152 us (0.89)
  Pallas kernels: 162 us -> 144 us
    pallas_call x1, Pallas kernels: 162 us -> 144 us  [shards(): pl.pallas_call(functools.partial(kernel, crops, groups), out_shape=(jax.S...]
where the time goes in v4:
time: 152 us; the launch traced here: 151 us
  Pallas kernels  144 us (95%)
  local copies, waits for them, and re-layouts  7.11 us (5%)
    pallas_call x1, Pallas kernels, shards(): pl.pallas_call(functools.partial(kernel, crops, groups), out_shape=(jax.S...  144 us
    unnamed x19, local copies, waits for them, and re-layouts  7.11 us

profile of v4, /device:TPU:0, one launch (start us, length us, event | category | flops | bytes accessed | tf_op | source)
XLA Modules:
  0.0 151.4 jit_solution(9646851978909355606)
XLA Ops:
  0.6 143.6 %tri.1 = (bf16[32,128,128]{2,1,0:T(8,128)(2,1)}, bf16[32,128,128]{2,1,0:T(8,128)(2,1)}, f32[128,512]{1,0:T(8,128)}, f32[128,128]{1,0:T(8,128)}, f32[128,128]{1,0...) custom-call(bf16[32,128,128]{2,1,0:T(8,128)(2,1)} %bitcast.10, bf16[32,128,128]{2,1,0:T(8,128)(2,1)} %bitcast.11, ...), custom_call_target="tpu_custom_call" | custom-call | tf_op jit(solution)/shard_map/tri/pallas_call | solution.py:500
  144.3 0.0 copy-start
  144.3 2.4 %copy.23 = bf16[1,32,128,128]{3,2,1,0:T(8,128)(2,1)} copy(bf16[1,32,128,128]{3,2,1,0:T(8,128)(2,1)} %bitcast.9) | data formatting | bytes 2097152
  146.7 0.0 copy-done
  146.7 0.0 copy-start.1
  146.7 1.0 copy.24
  147.6 0.1 copy-done.1
  147.8 0.0 copy-start.3
  147.8 0.7 copy.25
  148.5 0.2 copy-done.3
  148.6 0.0 copy-start.2
  148.6 0.6 copy.26
  149.3 0.2 copy-done.2
  149.5 0.0 copy-start.5
  149.5 0.6 copy.27
  150.1 0.0 copy-done.5
  150.2 0.0 copy-start.4
  150.2 0.6 copy.28
  150.7 0.1 copy-done.4
  150.8 0.6 copy.29
Async XLA Ops:
  144.3 2.4 %copy-start = (bf16[32,128,128]{2,1,0:T(8,128)(2,1)S(1)}, bf16[32,128,128]{2,1,0:T(8,128)(2,1)}, u32[]{:S(2)}) copy-start(bf16[32,128,128]{2,1,0:T(8,128)(2,1)} %get-tuple-element.15) | copy-start | bytes 3145732
  146.7 1.1 copy-start.1
  147.8 0.9 copy-start.3
  148.6 0.9 copy-start.2
  149.5 0.7 copy-start.5
  150.2 0.7 copy-start.4
